TPU v7x, 256 devices: a whole 4x4x8 slice. The times are simulated.
256 devices in a mesh: dp: 32 (over z, y_hi, core), mp: 8 (over x, y_lo).
Axes of the slice: x: 4, y: 4 (y_hi: 2, y_lo: 2; y = y_hi * 2 + y_lo), z: 8, core: 2. Of those that a mesh axis runs over, the one named last changes fastest.
Arguments:
- token_ids: int32 [128, 64], P(None, 'dp'), may hold values from 0 to 1023
- fanout: int32 [128, 16], replicated, may hold values from 1 to 16
- table_of_column: int32 [64], P('dp'), may hold values from 0 to 15
- embed_table: bfloat16 [64, 1024, 1024], P('dp', 'mp'), may hold values from -35 to 35
- start_vector: bfloat16 [1024], replicated, may hold values from -6 to 6
- gain_attn: bfloat16 [1024], replicated, may hold values from 0.25 to 1.75
- gain_mlp: bfloat16 [1024], replicated, may hold values from 0.25 to 1.75
- gain_final: bfloat16 [1024], replicated, may hold values from 0.25 to 1.75
- w_qkv: bfloat16 [1024, 3, 1024], P(None, None, 'mp'), may hold values from -8 to 8
- w_out: bfloat16 [1024, 1024], P(None, 'mp'), may hold values from -0.1875 to 0.1875
- w_gate: bfloat16 [1024, 4096], P(None, 'mp'), may hold values from -0.1875 to 0.1875
- w_up: bfloat16 [1024, 4096], P(None, 'mp'), may hold values from -0.1875 to 0.1875
- w_down: bfloat16 [1024, 4096], P(None, 'mp'), may hold values from -0.09375 to 0.09375
Outputs:
- nll: float32 [128, 64], P(None, 'dp')
- grad_table: float32 [64, 1024, 1024], P('dp', 'mp')
- grad_qkv: float32 [1024, 3, 1024], P('dp', None, 'mp')
- grad_out: float32 [1024, 1024], P('dp', 'mp')
- grad_gate: float32 [1024, 4096], P('dp', 'mp')
- grad_up: float32 [1024, 4096], P('dp', 'mp')
- grad_down: float32 [1024, 4096], P('dp', 'mp')
All inputs are finite; a program needn't handle non-finite values.
Results may differ from a plain program's by a relative error of at most 0.015.
The roundings to bfloat16 on the way count: a program that leaves them out, or rounds other values in their place, can miss the bound.
Values may be sent and summed in bfloat16 or wider, within the bound.
A program may use at most 128 MiB of HBM per device.

v0:
```python
import math
import jax
import jax.numpy as jnp
from jax import lax
from jax.sharding import PartitionSpec as P

HS = 64
TABLES = 16
EPS = 1e-05
ATTN_CAP = 50.0
LOGIT_CAP = 30.0


def gather_features(values):
    return lax.all_gather(values, "mp", axis=2, tiled=True)


def feature_sum(term):
    return lax.psum_scatter(term, "mp", scatter_dimension=2, tiled=True)


def cols_to_rows(values):
    return lax.all_to_all(values, "dp", split_axis=0, concat_axis=1, tiled=True)


def rows_to_cols(values):
    return lax.all_to_all(values, "dp", split_axis=1, concat_axis=0, tiled=True)


def rms_of(values):
    floats = values.astype(jnp.float32)
    return jnp.sqrt(jnp.mean(floats * floats, axis=-1, keepdims=True) + EPS)


def normalize(values, gain, rms):
    return (values.astype(jnp.float32) / rms * gain.astype(jnp.float32)).astype(jnp.bfloat16)


def norm_back_full(values, d_norm, gain, rms):
    floats = values.astype(jnp.float32)
    gains = gain.astype(jnp.float32)
    total = jnp.sum(gains * d_norm * floats, axis=-1, keepdims=True)
    return gains * d_norm / rms - floats * total / (floats.shape[-1] * rms * rms * rms)


def norm_back_part(values, d_norm, gain, rms, model_width):
    floats = values.astype(jnp.float32)
    gains = gain.astype(jnp.float32)
    partial_total = jnp.sum(gains * d_norm * floats, axis=-1)
    total = lax.psum(partial_total, "mp")[..., None]
    return gains * d_norm / rms - floats * total / (model_width * rms * rms * rms)


def local(
    token_ids,
    fanout,
    table_of_column,
    embed_table,
    start_vector,
    gain_attn,
    gain_mlp,
    gain_final,
    w_qkv,
    w_out,
    w_gate,
    w_up,
    w_down,
):
    fl = jnp.float32
    mp_rank = lax.axis_index("mp")
    mp_count = lax.axis_size("mp")
    model_width = embed_table.shape[2]
    vocab_part = embed_table.shape[1]
    part_width = model_width // mp_count
    head_cols = w_qkv.shape[2]
    local_heads = head_cols // HS
    row_total_count = token_ids.shape[0]

    def own_part(vector):
        return lax.dynamic_slice_in_dim(vector, mp_rank * part_width, part_width, 0)

    local_ids = token_ids - mp_rank * vocab_part
    onehot = (
        local_ids[:, :, None] == jnp.arange(vocab_part, dtype=jnp.int32)[None, None, :]
    ).astype(jnp.bfloat16)
    picked = jnp.einsum("rcv,cvd->rcd", onehot, embed_table, preferred_element_type=fl)
    emb_cols = feature_sum(picked).astype(jnp.bfloat16)
    emb_rows = cols_to_rows(emb_cols)
    rows_here = emb_rows.shape[0]
    col_count = emb_rows.shape[1]
    start_rows = jnp.broadcast_to(own_part(start_vector)[None, None, :], (rows_here, 1, part_width))
    resid_in = jnp.concatenate([start_rows, emb_rows[:, :-1]], axis=1)
    in_full = gather_features(resid_in)
    rms_attn = rms_of(in_full)
    norm_attn = normalize(in_full, gain_attn, rms_attn)
    qkv = jnp.einsum("rpd,dtx->rptx", norm_attn, w_qkv, preferred_element_type=fl).astype(
        jnp.bfloat16
    )
    queries = qkv[:, :, 0].reshape(rows_here, col_count, local_heads, HS)
    key_rows = qkv[:, :, 1].reshape(rows_here, col_count, local_heads, HS)
    value_rows = qkv[:, :, 2].reshape(rows_here, col_count, local_heads, HS)
    score_raw = jnp.einsum(
        "rqhe,rkhe->rhqk", queries, key_rows, preferred_element_type=fl
    ) / math.sqrt(HS)
    score = ATTN_CAP * jnp.tanh(score_raw / ATTN_CAP)
    col_index = jnp.arange(col_count, dtype=jnp.int32)
    causal = col_index[:, None] >= col_index[None, :]
    exp_score = jnp.where(causal, jnp.exp(score), 0.0)
    attn_prob = exp_score / jnp.sum(exp_score, axis=-1, keepdims=True)
    prob_b = attn_prob.astype(jnp.bfloat16)
    attn_heads = jnp.einsum(
        "rhqk,rkhe->rqhe", prob_b, value_rows, preferred_element_type=fl
    ).astype(jnp.bfloat16)
    attn_out = attn_heads.reshape(rows_here, col_count, head_cols)
    mixed_part = jnp.einsum("rpj,dj->rpd", attn_out, w_out, preferred_element_type=fl)
    resid_mid = (resid_in.astype(fl) + feature_sum(mixed_part)).astype(jnp.bfloat16)
    mid_full = gather_features(resid_mid)
    rms_mlp = rms_of(mid_full)
    norm_mlp = normalize(mid_full, gain_mlp, rms_mlp)
    gate_pre = jnp.einsum("rpd,df->rpf", norm_mlp, w_gate, preferred_element_type=fl)
    up_proj = jnp.einsum("rpd,df->rpf", norm_mlp, w_up, preferred_element_type=fl)
    hidden = (jax.nn.silu(gate_pre) * up_proj).astype(jnp.bfloat16)
    down_part = jnp.einsum("rpf,df->rpd", hidden, w_down, preferred_element_type=fl)
    resid_out = (resid_mid.astype(fl) + feature_sum(down_part)).astype(jnp.bfloat16)
    out_cols = rows_to_cols(resid_out)
    out_full = gather_features(out_cols)
    rms_final = rms_of(out_full)
    norm_final = normalize(out_full, gain_final, rms_final)
    width_root = math.sqrt(model_width)
    logit_raw = (
        jnp.einsum("rcd,cvd->rcv", norm_final, embed_table, preferred_element_type=fl) / width_root
    )
    capped = LOGIT_CAP * jnp.tanh(logit_raw / LOGIT_CAP)
    exp_logit = jnp.exp(capped)
    onehot_f = onehot.astype(fl)
    exp_total, target_logit = lax.psum(
        (jnp.sum(exp_logit, axis=-1), jnp.sum(capped * onehot_f, axis=-1)), "mp"
    )
    nll = jnp.log(exp_total) - target_logit
    select = table_of_column[None, :, None] == jnp.arange(TABLES, dtype=jnp.int32)[None, None, :]
    counts = jnp.sum(jnp.where(select, fanout[:, None, :], 0), axis=-1).astype(fl)
    row_scale = 1.0 / (counts * row_total_count)
    ratio = capped / LOGIT_CAP
    d_logit = (
        (exp_logit / exp_total[:, :, None] - onehot_f)
        * row_scale[:, :, None]
        * (1.0 - ratio * ratio)
    ).astype(jnp.bfloat16)
    d_final_part = (
        jnp.einsum("rcv,cvd->rcd", d_logit, embed_table, preferred_element_type=fl) / width_root
    )
    table_grad = (
        jnp.einsum("rcv,rcd->cvd", d_logit, norm_final, preferred_element_type=fl) / width_root
    )
    d_final = lax.psum(d_final_part, "mp")
    back_full = norm_back_full(out_full, d_final, gain_final, rms_final)
    d_out_cols = lax.dynamic_slice_in_dim(back_full, mp_rank * part_width, part_width, 2).astype(
        jnp.bfloat16
    )
    d_out = cols_to_rows(d_out_cols)
    d_out_full = gather_features(d_out)
    d_hidden = jnp.einsum("rpd,df->rpf", d_out_full, w_down, preferred_element_type=fl)
    sigmoid_gate = jax.nn.sigmoid(gate_pre)
    d_gate = (d_hidden * up_proj * sigmoid_gate * (1.0 + gate_pre * (1.0 - sigmoid_gate))).astype(
        jnp.bfloat16
    )
    d_up = (d_hidden * gate_pre * sigmoid_gate).astype(jnp.bfloat16)
    d_norm_mlp = jnp.einsum("rpf,df->rpd", d_gate, w_gate, preferred_element_type=fl) + jnp.einsum(
        "rpf,df->rpd", d_up, w_up, preferred_element_type=fl
    )
    d_mid = (
        d_out.astype(fl)
        + norm_back_part(
            resid_mid, feature_sum(d_norm_mlp), own_part(gain_mlp), rms_mlp, model_width
        )
    ).astype(jnp.bfloat16)
    mid_grad_full = gather_features(d_mid)
    d_attn = jnp.einsum("rpd,dj->rpj", mid_grad_full, w_out, preferred_element_type=fl).astype(
        jnp.bfloat16
    )
    d_attn = d_attn.reshape(rows_here, col_count, local_heads, HS)
    d_prob = jnp.einsum("rqhe,rkhe->rhqk", d_attn, value_rows, preferred_element_type=fl)
    ratio_s = score / ATTN_CAP
    d_score = attn_prob * (d_prob - jnp.sum(attn_prob * d_prob, axis=-1, keepdims=True))
    d_scaled = (d_score * (1.0 - ratio_s * ratio_s) / math.sqrt(HS)).astype(jnp.bfloat16)
    d_query = jnp.einsum("rhqk,rkhe->rqhe", d_scaled, key_rows, preferred_element_type=fl)
    d_key = jnp.einsum("rhqk,rqhe->rkhe", d_scaled, queries, preferred_element_type=fl)
    d_value = jnp.einsum("rhqk,rqhe->rkhe", prob_b, d_attn, preferred_element_type=fl)
    d_qkv = (
        jnp.stack([d_query, d_key, d_value], axis=2)
        .reshape(rows_here, col_count, 3, head_cols)
        .astype(jnp.bfloat16)
    )
    d_norm_attn = jnp.einsum("rptx,dtx->rpd", d_qkv, w_qkv, preferred_element_type=fl)
    d_in = (
        d_mid.astype(fl)
        + norm_back_part(
            resid_in, feature_sum(d_norm_attn), own_part(gain_attn), rms_attn, model_width
        )
    ).astype(jnp.bfloat16)
    d_embed_rows = jnp.concatenate(
        [d_in[:, 1:], jnp.zeros((rows_here, 1, part_width), jnp.bfloat16)], axis=1
    )
    d_embed_cols = rows_to_cols(d_embed_rows)
    d_embed_full = gather_features(d_embed_cols)
    table_grad = table_grad + jnp.einsum(
        "rcv,rcd->cvd", onehot, d_embed_full, preferred_element_type=fl
    )
    qkv_term = jnp.einsum("rpd,rptx->dtx", norm_attn, d_qkv, preferred_element_type=fl).reshape(
        model_width, 3 * head_cols
    )
    out_term = jnp.einsum("rpd,rpj->dj", mid_grad_full, attn_out, preferred_element_type=fl)
    whole_terms = jnp.concatenate(
        [
            jnp.concatenate([qkv_term, out_term], axis=1),
            jnp.concatenate(
                [
                    jnp.einsum("rpd,rpf->df", norm_mlp, d_gate, preferred_element_type=fl),
                    jnp.einsum("rpd,rpf->df", norm_mlp, d_up, preferred_element_type=fl),
                    jnp.einsum("rpd,rpf->df", d_out_full, hidden, preferred_element_type=fl),
                ],
                axis=1,
            ),
        ],
        axis=1,
    )
    summed = lax.psum_scatter(whole_terms, "dp", scatter_dimension=0, tiled=True)
    ff_part = w_gate.shape[1]
    qkv_width = 3 * head_cols
    grad_qkv = summed[:, :qkv_width].reshape(summed.shape[0], 3, head_cols)
    grad_out = summed[:, qkv_width : qkv_width + head_cols]
    base = qkv_width + head_cols
    grad_gate = summed[:, base : base + ff_part]
    grad_up = summed[:, base + ff_part : base + 2 * ff_part]
    grad_down = summed[:, base + 2 * ff_part : base + 3 * ff_part]
    return (nll, table_grad, grad_qkv, grad_out, grad_gate, grad_up, grad_down)


def solution(mesh):
    return jax.shard_map(
        local,
        mesh=mesh,
        in_specs=(
            P(None, "dp"),
            P(),
            P("dp"),
            P("dp", "mp", None),
            P(),
            P(),
            P(),
            P(),
            P(None, None, "mp"),
            P(None, "mp"),
            P(None, "mp"),
            P(None, "mp"),
            P(None, "mp"),
        ),
        out_specs=(
            P(None, "dp"),
            P("dp", "mp", None),
            P("dp", None, "mp"),
            P("dp", "mp"),
            P("dp", "mp"),
            P("dp", "mp"),
            P("dp", "mp"),
        ),
        check_vma=False,
    )
```

profile of v0, /device:TPU:2, one launch (start us, length us, event | category | flops | bytes accessed | tf_op | source)
XLA Modules:
  0.0 726.3 jit_solution(7134462608592402723)
XLA Ops:
  8.0 2.4 convolution_bitcast_fusion
  10.4 44.1 %reduce-scatter.9.cloned.1.call-done = f32[128,2,128]{2,0,1:T(8,128)} async-done(((f32[128,2,1024]{2,0,1:T(8,128)}), f32[128,2,128]{2,0,1:T(8,128)}) %reduce-scatter.9.cloned.1.call-update) | async-done | bytes 131088 | tf_op jit(solution)/shard_map/reduce_scatter | solution.py:19
  54.5 0.9 convert_element_type.114
  56.1 10.0 %all-to-all-start = ((bf16[128,2,128]{2,1,0:T(2,128)(2,1)}), bf16[128,2,128]{2,1,0:T(2,128)(2,1)S(1)}, u32[]{:S(2)}, u32[]{:S(2)}) async-start(bf16[128,2,128]{2,1,0:T(2,128)(2,1)} %copy.114), calls=%async_computation.1 | async-start | bytes 131072 | tf_op jit(solution)/shard_map/all_to_all | solution.py:23
  67.7 8.4 %all-to-all-done = bf16[128,2,128]{2,1,0:T(2,128)(2,1)S(1)} async-done(((bf16[128,2,128]{2,1,0:T(2,128)(2,1)}), bf16[128,2,128]{2,1,0:T(2,128)(2,1)S(1)}, u32[]{:S(2)}, u32[]{:S(2)}) %all-to-all-start) | async-done | bytes 65568 | tf_op jit(solution)/shard_map/all_to_all | solution.py:23
  76.8 26.7 %all_gather.18 = bf16[4,64,1024]{2,1,0:T(8,128)(2,1)S(1)} all-gather(bf16[4,64,128]{2,1,0:T(8,128)(2,1)S(1)} %get-tuple-element.52), channel_id=1, replica_groups=mesh['dp'=32,'mp'=8] {'mp'}, dimensions={2}, use_global_device_ids=true | all-gather | bytes 589824 | tf_op jit(solution)/shard_map/all_gather | solution.py:15
  104.3 1.6 convolution_convert_fusion
  107.0 1.3 fusion.35
  108.4 34.5 %reduce-scatter.11.cloned.1.call-done = f32[4,64,128]{2,1,0:T(8,128)} async-done(((f32[4,64,1024]{2,1,0:T(8,128)}), f32[4,64,128]{2,1,0:T(8,128)}) %reduce-scatter.11.cloned.1.call-update) | async-done | bytes 131088 | tf_op jit(solution)/shard_map/reduce_scatter | solution.py:19
  142.9 0.9 add_convert_fusion
  143.8 26.9 %all_gather.19 = bf16[4,64,1024]{2,1,0:T(8,128)(2,1)S(1)} all-gather(bf16[4,64,128]{2,1,0:T(8,128)(2,1)S(1)} %add_convert_fusion), channel_id=1, replica_groups=mesh['dp'=32,'mp'=8] {'mp'}, dimensions={2}, use_global_device_ids=true | all-gather | bytes 589824 | tf_op jit(solution)/shard_map/all_gather | solution.py:15
  171.5 1.8 fusion.25
  173.3 0.8 copy-done.40
  174.1 2.5 multiply_convert_fusion.3
  176.7 1.4 fusion.18
  178.3 40.9 %reduce-scatter.13.cloned.1.call-done = f32[4,64,128]{2,1,0:T(8,128)} async-done(((f32[4,64,1024]{2,1,0:T(8,128)}), f32[4,64,128]{2,1,0:T(8,128)}) %reduce-scatter.13.cloned.1.call-update) | async-done | bytes 131088 | tf_op jit(solution)/shard_map/reduce_scatter | solution.py:19
  219.3 0.9 fusion.45
  220.9 10.0 %all-to-all-start.1 = ((bf16[4,64,128]{2,0,1:T(4,128)(2,1)}), bf16[4,64,128]{2,0,1:T(4,128)(2,1)S(1)}, u32[]{:S(2)}, u32[]{:S(2)}) async-start(bf16[4,64,128]{2,0,1:T(4,128)(2,1)} %copy.121), calls=%async_computation.4 | async-start | bytes 131072 | tf_op jit(solution)/shard_map/all_to_all | solution.py:27
  231.5 9.3 %all-to-all-done.1 = bf16[4,64,128]{2,0,1:T(4,128)(2,1)S(1)} async-done(((bf16[4,64,128]{2,0,1:T(4,128)(2,1)}), bf16[4,64,128]{2,0,1:T(4,128)(2,1)S(1)}, u32[]{:S(2)}, u32[]{:S(2)}) %all-to-all-start.1) | async-done | bytes 65568 | tf_op jit(solution)/shard_map/all_to_all | solution.py:27
  240.9 26.7 %all_gather.20 = bf16[128,2,1024]{2,0,1:T(8,128)(2,1)S(1)} all-gather(bf16[128,2,128]{2,0,1:T(8,128)(2,1)S(1)} %bitcast.144), channel_id=1, replica_groups=mesh['dp'=32,'mp'=8] {'mp'}, dimensions={2}, use_global_device_ids=true | all-gather | bytes 589824 | tf_op jit(solution)/shard_map/all_gather | solution.py:15
  268.3 1.6 fusion.63
  269.9 14.4 %psum.35 = f32[128,2]{0,1:T(2,128)S(1)} all-reduce(f32[128,2]{0,1:T(2,128)} %get-tuple-element.35), channel_id=1, replica_groups=mesh['dp'=32,'mp'=8] {'mp'}, use_global_device_ids=true, to_apply=%region_8.9 | all-reduce | flops 256 | bytes 2048 | tf_op jit(solution)/shard_map/psum | solution.py:136
  284.3 2.2 fusion.1
  286.6 1.1 convert_element_type.130
  287.8 76.1 %all-reduce.4.cloned.1.call-done = f32[128,2,1024]{2,0,1:T(8,128)} async-done(((f32[128,2,1024]{2,0,1:T(8,128)}), f32[128,2,1024]{2,0,1:T(8,128)}) %all-reduce.4.cloned.1.call-update) | async-done | bytes 1048592 | tf_op jit(solution)/shard_map/psum | solution.py:155
  363.9 1.6 multiply_reduce_fusion
  365.5 1.1 fusion.54
  366.6 19.4 %all_to_all.72 = bf16[128,2,128]{2,1,0:T(2,128)(2,1)S(1)} all-to-all(bf16[128,2,128]{2,1,0:T(2,128)(2,1)S(1)} %copy.124), channel_id=1, replica_groups=mesh['dp'=32,'mp'=8] {'dp'}, dimensions={0} | all-to-all | bytes 131072 | tf_op jit(solution)/shard_map/all_to_all | solution.py:23
  386.1 26.0 %all_gather.21 = bf16[4,64,1024]{2,1,0:T(8,128)(2,1)S(1)} all-gather(bf16[4,64,128]{2,1,0:T(8,128)(2,1)S(1)} %bitcast.138), channel_id=1, replica_groups=mesh['dp'=32,'mp'=8] {'mp'}, dimensions={2}, use_global_device_ids=true | all-gather | bytes 589824 | tf_op jit(solution)/shard_map/all_gather | solution.py:15
  412.1 1.9 multiply_convert_fusion.1
  414.8 1.4 convolution_add_fusion.1
  416.3 1.3 dynamic-slice_convert_fusion.1
  417.6 33.3 %reduce-scatter.15.cloned.1.call-done = f32[4,64,128]{2,1,0:T(8,128)} async-done(((f32[4,64,1024]{2,1,0:T(8,128)}), f32[4,64,128]{2,1,0:T(8,128)}) %reduce-scatter.15.cloned.1.call-update) | async-done | bytes 131088 | tf_op jit(solution)/shard_map/reduce_scatter | solution.py:19
  450.9 1.6 fusion.46
  452.5 18.0 %psum.38 = f32[4,64]{1,0:T(4,128)} all-reduce(f32[4,64]{1,0:T(4,128)} %fusion.46), channel_id=1, replica_groups=mesh['dp'=32,'mp'=8] {'mp'}, use_global_device_ids=true, to_apply=%region_16.17 | all-reduce | flops 256 | bytes 2048 | tf_op jit(solution)/shard_map/psum | solution.py:50
  470.5 1.1 fusion.61
  472.2 27.0 %all_gather.22 = bf16[4,64,1024]{2,1,0:T(8,128)(2,1)S(1)} all-gather(bf16[4,64,128]{2,1,0:T(8,128)(2,1)S(1)} %fusion.61), channel_id=1, replica_groups=mesh['dp'=32,'mp'=8] {'mp'}, dimensions={2}, use_global_device_ids=true | all-gather | bytes 589824 | tf_op jit(solution)/shard_map/all_gather | solution.py:15
  499.2 0.9 convolution_convert_fusion.5
  500.1 1.0 copy.166
  501.1 1.8 fusion.65
  502.9 1.8 convolution_convert_fusion.1
  504.7 1.6 convolution_convert_fusion.3
  506.3 2.2 convolution_convert_fusion.2
  508.5 1.0 copy.136
  509.5 1.0 copy.135
  510.7 2.6 convolution_bitcast_fusion.1
  513.6 2.7 bitcast_dynamic-update-slice_fusion.3
  516.2 2.0 fusion.2
  518.2 2.8 bitcast_dynamic-update-slice_fusion.2
  521.1 2.6 bitcast_dynamic-update-slice_fusion.1
  523.7 1.8 bitcast_dynamic-update-slice_fusion
  525.4 9.2 %copy.156 = f32[1024,2048]{1,0:T(8,128)} copy(f32[1024,2048]{0,1:T(8,128)} %bitcast_dynamic-update-slice_fusion) | data formatting | bytes 16777216
  534.7 0.9 dynamic-slice_convert_fusion
  535.7 1.5 convolution_multiply_fusion.1
  537.2 17.6 %reduce-scatter.17.cloned.1.call-done = f32[4,64,128]{2,1,0:T(8,128)} async-done(((f32[4,64,1024]{2,1,0:T(8,128)}), f32[4,64,128]{2,1,0:T(8,128)}) %reduce-scatter.17.cloned.1.call-update) | async-done | bytes 131088 | tf_op jit(solution)/shard_map/reduce_scatter | solution.py:19
  554.8 1.0 multiply_reduce_fusion.3
  555.9 17.3 %all-reduce.1 = (f32[128,2]{0,1:T(2,128)S(1)}, f32[4,64]{1,0:T(4,128)S(1)}) all-reduce(f32[128,2]{0,1:T(2,128)S(1)} %copy-done.36, f32[4,64]{1,0:T(4,128)S(1)} %get-tuple-element.39), channel_id=1, replica_groups=mesh['dp'=32,'mp'=8] {'mp'}, use_global_device_ids=true, to_apply=%region_10.11 | all-reduce | flops 512 | bytes 4096 | tf_op jit(solution)/shard_map/psum | solution.py:136
  574.1 10.0 %all-to-all-start.3 = ((bf16[4,64,128]{2,0,1:T(4,128)(2,1)}), bf16[4,64,128]{2,0,1:T(4,128)(2,1)S(1)}, u32[]{:S(2)}, u32[]{:S(2)}) async-start(bf16[4,64,128]{2,0,1:T(4,128)(2,1)} %concatenate.12.clone), calls=%async_computation.8 | async-start | bytes 131072 | tf_op jit(solution)/shard_map/all_to_all | solution.py:27
  584.6 9.4 %all-to-all-done.3 = bf16[4,64,128]{2,0,1:T(4,128)(2,1)S(1)} async-done(((bf16[4,64,128]{2,0,1:T(4,128)(2,1)}), bf16[4,64,128]{2,0,1:T(4,128)(2,1)S(1)}, u32[]{:S(2)}, u32[]{:S(2)}) %all-to-all-start.3) | async-done | bytes 65568 | tf_op jit(solution)/shard_map/all_to_all | solution.py:27
  594.0 28.0 %all_gather.23 = bf16[128,2,1024]{2,0,1:T(8,128)(2,1)S(1)} all-gather(bf16[128,2,128]{2,0,1:T(8,128)(2,1)S(1)} %bitcast.145), channel_id=1, replica_groups=mesh['dp'=32,'mp'=8] {'mp'}, dimensions={2}, use_global_device_ids=true | all-gather | bytes 589824 | tf_op jit(solution)/shard_map/all_gather | solution.py:15
  622.0 2.5 convolution_add_fusion
  624.5 90.4 %reduce-scatter.19.cloned.1.call-done = f32[32,2048]{1,0:T(8,128)} async-done(((f32[1024,2048]{1,0:T(8,128)}), f32[32,2048]{1,0:T(8,128)}) %reduce-scatter.19.cloned.1.call-update) | async-done | bytes 262160
  716.6 1.3 slice.51
  717.9 1.6 fusion.94
  (137 shorter events, 14.1 us)
Async XLA Ops:
  7.2 169.5 %copy-start = (bf16[1024,512]{1,0:T(8,128)(2,1)S(1)}, bf16[1024,512]{1,0:T(8,128)(2,1)}, u32[]{:S(2)}) copy-start(bf16[1024,512]{1,0:T(8,128)(2,1)} %param.25) | copy-start | bytes 3145732
  7.2 99.8 %copy-start.6 = (bf16[1024,128]{1,0:T(8,128)(2,1)S(1)}, bf16[1024,128]{1,0:T(8,128)(2,1)}, u32[]{:S(2)}) copy-start(bf16[1024,128]{1,0:T(8,128)(2,1)} %param.22) | copy-start | bytes 786436
  7.2 101.1 %copy-start.35 = (bf16[1024]{0:T(1024)(128)(2,1)S(1)}, bf16[1024]{0:T(1024)(128)(2,1)}, u32[]{:S(2)}) copy-start(bf16[1024]{0:T(1024)(128)(2,1)} %param.19) | copy-start | bytes 6148
  7.2 47.3 %reduce-scatter.9.cloned.1.call-start = ((), (), s32[]{:S(2)}) async-start(), calls=%async_computation.10 | async-start | bytes 1179648 | tf_op jit(solution)/shard_map/reduce_scatter | solution.py:19
  56.1 20.0 %all-to-all-start = ((bf16[128,2,128]{2,1,0:T(2,128)(2,1)}), bf16[128,2,128]{2,1,0:T(2,128)(2,1)S(1)}, u32[]{:S(2)}, u32[]{:S(2)}) async-start(bf16[128,2,128]{2,1,0:T(2,128)(2,1)} %copy.114), calls=%async_computation.1 | async-start | bytes 131072 | tf_op jit(solution)/shard_map/all_to_all | solution.py:23
  66.1 76.7 %reduce-scatter.11.cloned.1.call-start = ((), (), s32[]{:S(2)}) async-start(), calls=%async_computation.11 | async-start | bytes 1179648 | tf_op jit(solution)/shard_map/reduce_scatter | solution.py:19
  66.9 39.3 %copy-start.30 = (f32[1024]{0:T(1024)}, f32[1024]{0:T(1024)S(1)}, u32[]{:S(2)}) copy-start(f32[1024]{0:T(1024)S(1)} %convert_element_type.117) | copy-start | bytes 12292
  67.7 76.2 %copy-start.28 = (pred[64,64]{0,1:T(8,128)(4,1)}, pred[64,64]{0,1:T(8,128)(4,1)S(1)}, u32[]{:S(2)}) copy-start(pred[64,64]{0,1:T(8,128)(4,1)S(1)} %iota_compare_fusion.3) | copy-start | bytes 12292
  104.3 1.9 copy-start.25
  106.1 36.8 %copy-start.21 = (bf16[4,64,1,128]{1,3,0,2:T(8,128)(2,1)}, bf16[4,64,1,128]{1,3,0,2:T(8,128)(2,1)S(1)}, u32[]{:S(2)}) copy-start(bf16[4,64,1,128]{1,3,0,2:T(8,128)(2,1)S(1)} %copy.165) | copy-start | bytes 196612
  106.2 36.7 %copy-start.13 = (bf16[4,64,2,64]{3,2,1,0:T(2,128)(2,1)}, bf16[4,64,2,64]{3,2,1,0:T(2,128)(2,1)S(1)}, u32[]{:S(2)}) copy-start(bf16[4,64,2,64]{3,2,1,0:T(2,128)(2,1)S(1)} %reshape_squeeze.9) | copy-start | bytes 196612
  106.4 36.5 %copy-start.22 = (bf16[4,64,1,128]{1,3,0,2:T(8,128)(2,1)}, bf16[4,64,1,128]{1,3,0,2:T(8,128)(2,1)S(1)}, u32[]{:S(2)}) copy-start(bf16[4,64,1,128]{1,3,0,2:T(8,128)(2,1)S(1)} %copy.164) | copy-start | bytes 196612
  106.7 1.6 copy-start.38
  106.7 64.0 %copy-start.39 = (f32[4,2,64]{2,1,0:T(2,128)}, f32[4,2,64]{2,1,0:T(2,128)S(1)}, u32[]{:S(2)}) copy-start(f32[4,2,64]{2,1,0:T(2,128)S(1)} %get-tuple-element.59) | copy-start | bytes 6148
  106.9 35.9 %copy-start.14 = (bf16[4,2,64,64]{3,2,1,0:T(8,128)(2,1)}, bf16[4,2,64,64]{3,2,1,0:T(8,128)(2,1)S(1)}, u32[]{:S(2)}) copy-start(bf16[4,2,64,64]{3,2,1,0:T(8,128)(2,1)S(1)} %convolution_convert_fusion.4) | copy-start | bytes 196612
  108.3 111.0 %reduce-scatter.13.cloned.1.call-start = ((), (), s32[]{:S(2)}) async-start(), calls=%async_computation.12 | async-start | bytes 1179648 | tf_op jit(solution)/shard_map/reduce_scatter | solution.py:19
  108.4 69.7 %copy-start.31 = (f32[1024]{0:T(1024)}, f32[1024]{0:T(1024)S(1)}, u32[]{:S(2)}) copy-start(f32[1024]{0:T(1024)S(1)} %convert_element_type.126) | copy-start | bytes 12292
  171.5 6.6 copy-start.23
  171.5 6.6 copy-start.34
  171.5 6.6 copy-start.37
  171.5 6.7 copy-start.27
  171.5 96.8 %copy-start.1 = (bf16[2,128,1024]{2,1,0:T(8,128)(2,1)S(1)}, bf16[2,128,1024]{2,1,0:T(8,128)(2,1)}, u32[]{:S(2)}) copy-start(bf16[2,128,1024]{2,1,0:T(8,128)(2,1)} %param.16) | copy-start | bytes 1572868
  173.3 0.8 copy-start.40
  176.7 64.2 %copy-start.7 = (bf16[4,64,512]{2,1,0:T(8,128)(2,1)}, bf16[4,64,512]{2,1,0:T(8,128)(2,1)S(1)}, u32[]{:S(2)}) copy-start(bf16[4,64,512]{2,1,0:T(8,128)(2,1)S(1)} %get-tuple-element.61) | copy-start | bytes 786436
  220.9 20.0 %all-to-all-start.1 = ((bf16[4,64,128]{2,0,1:T(4,128)(2,1)}), bf16[4,64,128]{2,0,1:T(4,128)(2,1)S(1)}, u32[]{:S(2)}, u32[]{:S(2)}) async-start(bf16[4,64,128]{2,0,1:T(4,128)(2,1)} %copy.121), calls=%async_computation.4 | async-start | bytes 131072 | tf_op jit(solution)/shard_map/all_to_all | solution.py:27
  230.9 133.0 %all-reduce.4.cloned.1.call-start = ((), (), s32[]{:S(2)}) async-start(), calls=%async_computation.13 | async-start | bytes 2097152 | tf_op jit(solution)/shard_map/psum | solution.py:155
  268.3 1.6 copy-start.32
  286.6 164.3 %reduce-scatter.15.cloned.1.call-start = ((), (), s32[]{:S(2)}) async-start(), calls=%async_computation.14 | async-start | bytes 1179648 | tf_op jit(solution)/shard_map/reduce_scatter | solution.py:19
  363.9 50.2 %copy-start.4 = (bf16[1024,512]{1,0:T(8,128)(2,1)S(1)}, bf16[1024,512]{1,0:T(8,128)(2,1)}, u32[]{:S(2)}) copy-start(bf16[1024,512]{1,0:T(8,128)(2,1)} %param.23) | copy-start | bytes 3145732
  363.9 51.0 %copy-start.5 = (bf16[1024,512]{1,0:T(8,128)(2,1)S(1)}, bf16[1024,512]{1,0:T(8,128)(2,1)}, u32[]{:S(2)}) copy-start(bf16[1024,512]{1,0:T(8,128)(2,1)} %param.24) | copy-start | bytes 3145732
  386.0 28.0 %copy-start.11 = (bf16[32,4,2,128]{3,2,0,1:T(2,128)(2,1)}, bf16[32,4,2,128]{3,2,0,1:T(2,128)(2,1)S(1)}, u32[]{:S(2)}) copy-start(bf16[32,4,2,128]{3,2,0,1:T(2,128)(2,1)S(1)} %copy.125) | copy-start | bytes 196612
  412.1 58.4 %copy-start.2 = (bf16[4,64,1024]{2,1,0:T(8,128)(2,1)}, bf16[4,64,1024]{2,1,0:T(8,128)(2,1)S(1)}, u32[]{:S(2)}) copy-start(bf16[4,64,1024]{2,1,0:T(8,128)(2,1)S(1)} %all_gather.21) | copy-start | bytes 1572868
  414.0 0.7 copy-start.15
  414.0 0.8 copy-start.18
  416.3 138.5 %reduce-scatter.17.cloned.1.call-start = ((), (), s32[]{:S(2)}) async-start(), calls=%async_computation.15 | async-start | bytes 1179648 | tf_op jit(solution)/shard_map/reduce_scatter | solution.py:19
  471.6 0.6 copy-start.9
  510.5 2.7 copy-start.16
  510.7 2.6 copy-start.17
  513.3 10.3 %copy-start.8 = (bf16[4,64,512]{2,1,0:T(8,128)(2,1)S(1)}, bf16[4,64,512]{2,1,0:T(8,128)(2,1)}, u32[]{:S(2)}) copy-start(bf16[4,64,512]{2,1,0:T(8,128)(2,1)} %copy-done.7) | copy-start | bytes 786436
  513.3 201.6 %reduce-scatter.19.cloned.1.call-start = ((), (), s32[]{:S(2)}) async-start(), calls=%async_computation.16 | async-start | bytes 8650752
  513.6 7.5 %copy-start.19 = (bf16[4,64,512]{2,1,0:T(8,128)(2,1)S(1)}, bf16[4,64,512]{2,1,0:T(8,128)(2,1)}, u32[]{:S(2)}) copy-start(bf16[4,64,512]{2,1,0:T(8,128)(2,1)} %copy-done.18) | copy-start | bytes 786436
  513.6 10.1 %copy-start.3 = (bf16[4,64,1024]{2,1,0:T(8,128)(2,1)S(1)}, bf16[4,64,1024]{2,1,0:T(8,128)(2,1)}, u32[]{:S(2)}) copy-start(bf16[4,64,1024]{2,1,0:T(8,128)(2,1)} %copy-done.2) | copy-start | bytes 1572868
  534.6 0.9 copy-start.26
  534.6 1.0 copy-start.24
  534.6 1.1 copy-start.20
  534.6 1.1 copy-start.29
  534.6 1.1 copy-start.33
  534.7 21.2 %copy-start.36 = (f32[128,2]{0,1:T(2,128)S(1)}, f32[128,2]{0,1:T(2,128)}, u32[]{:S(2)}) copy-start(f32[128,2]{0,1:T(2,128)} %get-tuple-element.36) | copy-start | bytes 3076
  534.7 38.5 %copy-start.10 = (bf16[4,64,128]{2,1,0:T(8,128)(2,1)S(1)}, bf16[4,64,128]{2,1,0:T(8,128)(2,1)}, u32[]{:S(2)}) copy-start(bf16[4,64,128]{2,1,0:T(8,128)(2,1)} %copy-done.9) | copy-start | bytes 196612
  534.7 38.5 %copy-start.12 = (f32[4,64,128]{2,1,0:T(8,128)S(1)}, f32[4,64,128]{2,1,0:T(8,128)}, u32[]{:S(2)}) copy-start(f32[4,64,128]{2,1,0:T(8,128)} %get-tuple-element.51) | copy-start | bytes 393220
  574.1 19.9 %all-to-all-start.3 = ((bf16[4,64,128]{2,0,1:T(4,128)(2,1)}), bf16[4,64,128]{2,0,1:T(4,128)(2,1)S(1)}, u32[]{:S(2)}, u32[]{:S(2)}) async-start(bf16[4,64,128]{2,0,1:T(4,128)(2,1)} %concatenate.12.clone), calls=%async_computation.8 | async-start | bytes 131072 | tf_op jit(solution)/shard_map/all_to_all | solution.py:27
Sparse Core Ops, SparseCore 0:
  11.1 43.3 reduce-scatter.8
  108.4 34.4 reduce-scatter.10
  178.3 40.9 reduce-scatter.12
  286.7 77.0 all-reduce.3
  416.4 34.4 reduce-scatter.14
  513.4 41.3 reduce-scatter.16
  559.2 155.6 reduce-scatter.18
where the time goes:
time: 728 us; the launch traced here: 726 us
  waiting for transfers between devices  364 us (50%)
  blocking collectives  230 us (32%)
  matrix products  46 us (6%)
  starting transfers between devices  30.4 us (4%)
  local copies, waits for them, and re-layouts  22.4 us (3%)
  other arithmetic  18.3 us (3%)
  between operations  14.7 us (2%)
    reduce_scatter x5, waiting for transfers between devices, feature_sum(): return lax.psum_scatter(term, 'mp', scatter_dimension=2, tiled=True)  170 us
    all_gather x6, blocking collectives, gather_features(): return lax.all_gather(values, 'mp', axis=2, tiled=True)  161 us
    unnamed x8, waiting for transfers between devices  90.5 us
    psum x1, waiting for transfers between devices, local(): d_final = lax.psum(d_final_part, 'mp')  76.1 us
    psum x2, blocking collectives, local(): lax.psum((jnp.sum(exp_logit, axis=-1), jnp.sum(capped * onehot_f, axis=-1...  31.7 us
    all_to_all x2, starting transfers between devices, rows_to_cols(): return lax.all_to_all(values, 'dp', split_axis=1, concat_axis=0, tiled=True)  20 us
    all_to_all x1, blocking collectives, cols_to_rows(): return lax.all_to_all(values, 'dp', split_axis=0, concat_axis=1, tiled=True)  19.4 us
    all_to_all x2, waiting for transfers between devices, rows_to_cols(): return lax.all_to_all(values, 'dp', split_axis=1, concat_axis=0, tiled=True)  18.7 us
  transfers between devices with their start and end apart: 10, of which 10 were waited for; matrix products, arithmetic and copies ran while one was open for 5% of the time, Pallas kernels for 0%

commit v1 on v0

--- a/solution.py
+++ b/solution.py
@@ -11,8 +11,15 @@
 LOGIT_CAP = 30.0
 
 
+def swapped_in(x, mesh_axis, d):
+    devices = lax.axis_size(mesh_axis)
+    parts = jnp.stack([x for _ in range(devices)])
+    parts = lax.all_to_all(parts, mesh_axis, split_axis=0, concat_axis=0)
+    return jnp.concatenate(parts, axis=d)
+
+
 def gather_features(values):
-    return lax.all_gather(values, "mp", axis=2, tiled=True)
+    return swapped_in(values, "mp", 2)
 
 
 def feature_sum(term):

time: 728 us -> 667 us (0.916)
  blocking collectives: 230 us -> 115 us
  waiting for transfers between devices: 364 us -> 401 us
  starting transfers between devices: 30.4 us -> 43.8 us
    all_gather x6 -> x0, blocking collectives: 161 us -> none  [gather_features(): return lax.all_gather(values, 'mp', axis=2, tiled=True)]
    all_to_all x0 -> x3, blocking collectives: none -> 44.3 us  [the longest x2 24.6 us: swapped_in(): parts = lax.all_to_all(parts, mesh_axis, split_axis=0, concat_axis=0)]
    all_to_all x0 -> x4, waiting for transfers between devices: none -> 29.3 us  [swapped_in(): parts = lax.all_to_all(parts, mesh_axis, split_axis=0, concat_axis=0)]
    all_to_all x0 -> x4, starting transfers between devices: none -> 23.6 us  [swapped_in(): parts = lax.all_to_all(parts, mesh_axis, split_axis=0, concat_axis=0)]
    unnamed x8, waiting for transfers between devices: 90.5 us -> 105 us
    all_to_all x2 -> x1, starting transfers between devices: 20 us -> 9.89 us  [rows_to_cols(): return lax.all_to_all(values, 'dp', split_axis=1, concat_axis=0, tiled=True)]
    all_to_all x2 -> x1, waiting for transfers between devices: 18.7 us -> 9.92 us  [rows_to_cols(): return lax.all_to_all(values, 'dp', split_axis=1, concat_axis=0, tiled=True)]
  transfers between devices with their start and end apart: 10 -> 13, of which waited for: 10 -> 13; matrix products, arithmetic and copies ran while one was open for 5% -> 5% of each run, Pallas kernels for 0% -> 0%
where the time goes in v1:
time: 667 us; the launch traced here: 665 us
  waiting for transfers between devices  401 us (60%)
  blocking collectives  115 us (17%)
  matrix products  45.7 us (7%)
  starting transfers between devices  43.8 us (7%)
  local copies, waits for them, and re-layouts  27.4 us (4%)
  other arithmetic  17.9 us (3%)
  between operations  14.6 us (2%)
    reduce_scatter x5, waiting for transfers between devices, feature_sum(): return lax.psum_scatter(term, 'mp', scatter_dimension=2, tiled=True)  173 us
    unnamed x8, waiting for transfers between devices  105 us
    psum x1, waiting for transfers between devices, local(): d_final = lax.psum(d_final_part, 'mp')  74.7 us
    psum x2, blocking collectives, local(): lax.psum((jnp.sum(exp_logit, axis=-1), jnp.sum(capped * onehot_f, axis=-1...  34.1 us
    all_to_all x4, waiting for transfers between devices, swapped_in(): parts = lax.all_to_all(parts, mesh_axis, split_axis=0, concat_axis=0)  29.3 us
    all_to_all x2, blocking collectives, swapped_in(): parts = lax.all_to_all(parts, mesh_axis, split_axis=0, concat_axis=0)  24.6 us
    all_to_all x4, starting transfers between devices, swapped_in(): parts = lax.all_to_all(parts, mesh_axis, split_axis=0, concat_axis=0)  23.6 us
    all_to_all x1, blocking collectives, rows_to_cols(): return lax.all_to_all(values, 'dp', split_axis=1, concat_axis=0, tiled=True)  19.6 us
  transfers between devices with their start and end apart: 13, of which 13 were waited for; matrix products, arithmetic and copies ran while one was open for 5% of the time, Pallas kernels for 0%

profile of v1, /device:TPU:2, one launch (start us, length us, event | category | flops | bytes accessed | tf_op | source)
XLA Modules:
  0.0 665.4 jit_solution(14718293753321374986)
XLA Ops:
  8.0 2.4 convolution_bitcast_fusion
  10.4 44.1 %reduce-scatter.9.cloned.1.call-done = f32[128,2,128]{2,0,1:T(8,128)} async-done(((f32[128,2,1024]{2,0,1:T(8,128)}), f32[128,2,128]{2,0,1:T(8,128)}) %reduce-scatter.9.cloned.1.call-update) | async-done | bytes 131088 | tf_op jit(solution)/shard_map/reduce_scatter | solution.py:26
  54.5 0.9 convert_element_type.144
  56.1 10.0 %all-to-all-start = ((bf16[128,2,128]{2,1,0:T(2,128)(2,1)}), bf16[128,2,128]{2,1,0:T(2,128)(2,1)S(1)}, u32[]{:S(2)}, u32[]{:S(2)}) async-start(bf16[128,2,128]{2,1,0:T(2,128)(2,1)} %copy.156), calls=%async_computation.1 | async-start | bytes 131072 | tf_op jit(solution)/shard_map/all_to_all | solution.py:30
  66.9 9.2 %all-to-all-done = bf16[128,2,128]{2,1,0:T(2,128)(2,1)S(1)} async-done(((bf16[128,2,128]{2,1,0:T(2,128)(2,1)}), bf16[128,2,128]{2,1,0:T(2,128)(2,1)S(1)}, u32[]{:S(2)}, u32[]{:S(2)}) %all-to-all-start) | async-done | bytes 65568 | tf_op jit(solution)/shard_map/all_to_all | solution.py:30
  77.7 5.7 all-to-all-start.1
  84.2 7.9 %all-to-all-done.1 = bf16[8,4,64,128]{3,2,1,0:T(8,128)(2,1)S(1)} async-done(((bf16[8,4,64,128]{3,2,1,0:T(8,128)(2,1)}), bf16[8,4,64,128]{3,2,1,0:T(8,128)(2,1)S(1)}, u32[]{:S(2)}, u32[]{:S(2)}) %all-to-all-start.1) | async-done | bytes 524320 | tf_op jit(solution)/shard_map/all_to_all | solution.py:17
  92.8 1.6 convolution_convert_fusion
  95.5 1.3 fusion.46
  96.8 34.7 %reduce-scatter.11.cloned.1.call-done = f32[4,64,128]{2,1,0:T(8,128)} async-done(((f32[4,64,1024]{2,1,0:T(8,128)}), f32[4,64,128]{2,1,0:T(8,128)}) %reduce-scatter.11.cloned.1.call-update) | async-done | bytes 131088 | tf_op jit(solution)/shard_map/reduce_scatter | solution.py:26
  131.5 0.9 add_convert_fusion
  133.3 6.1 all-to-all-start.2
  139.4 6.7 %all-to-all-done.2 = bf16[8,4,64,128]{3,2,1,0:T(8,128)(2,1)S(1)} async-done(((bf16[8,4,64,128]{3,2,1,0:T(8,128)(2,1)}), bf16[8,4,64,128]{3,2,1,0:T(8,128)(2,1)S(1)}, u32[]{:S(2)}, u32[]{:S(2)}) %all-to-all-start.2) | async-done | bytes 524320 | tf_op jit(solution)/shard_map/all_to_all | solution.py:17
  146.9 1.7 fusion.26
  148.6 2.7 multiply_convert_fusion.3
  151.4 1.4 fusion.19
  152.9 41.0 %reduce-scatter.13.cloned.1.call-done = f32[4,64,128]{2,1,0:T(8,128)} async-done(((f32[4,64,1024]{2,1,0:T(8,128)}), f32[4,64,128]{2,1,0:T(8,128)}) %reduce-scatter.13.cloned.1.call-update) | async-done | bytes 131088 | tf_op jit(solution)/shard_map/reduce_scatter | solution.py:26
  193.9 0.9 fusion.56
  195.5 9.9 %all-to-all-start.3 = ((bf16[4,64,128]{2,0,1:T(4,128)(2,1)}), bf16[4,64,128]{2,0,1:T(4,128)(2,1)S(1)}, u32[]{:S(2)}, u32[]{:S(2)}) async-start(bf16[4,64,128]{2,0,1:T(4,128)(2,1)} %copy.165), calls=%async_computation.6 | async-start | bytes 131072 | tf_op jit(solution)/shard_map/all_to_all | solution.py:34
  205.4 9.9 %all-to-all-done.3 = bf16[4,64,128]{2,0,1:T(4,128)(2,1)S(1)} async-done(((bf16[4,64,128]{2,0,1:T(4,128)(2,1)}), bf16[4,64,128]{2,0,1:T(4,128)(2,1)S(1)}, u32[]{:S(2)}, u32[]{:S(2)}) %all-to-all-start.3) | async-done | bytes 65568 | tf_op jit(solution)/shard_map/all_to_all | solution.py:34
  216.3 5.8 all-to-all-start.4
  223.4 7.2 %all-to-all-done.4 = bf16[8,128,2,128]{3,1,2,0:T(8,128)(2,1)S(1)} async-done(((bf16[8,128,2,128]{3,1,2,0:T(8,128)(2,1)}), bf16[8,128,2,128]{3,1,2,0:T(8,128)(2,1)S(1)}, u32[]{:S(2)}, u32[]{:S(2)}) %all-to-all-start.4) | async-done | bytes 524320 | tf_op jit(solution)/shard_map/all_to_all | solution.py:17
  231.4 1.6 fusion.74
  233.0 16.9 %psum.35 = f32[128,2]{0,1:T(2,128)S(1)} all-reduce(f32[128,2]{0,1:T(2,128)} %get-tuple-element.42), channel_id=1, replica_groups=mesh['dp'=32,'mp'=8] {'mp'}, use_global_device_ids=true, to_apply=%region_8.9 | all-reduce | flops 256 | bytes 2048 | tf_op jit(solution)/shard_map/psum | solution.py:143
  249.9 2.2 fusion.1
  252.2 1.1 copy_bitcast_fusion
  253.3 74.7 %all-reduce.4.cloned.1.call-done = f32[128,2,1024]{2,0,1:T(8,128)} async-done(((f32[128,2,1024]{2,0,1:T(8,128)}), f32[128,2,1024]{2,0,1:T(8,128)}) %all-reduce.4.cloned.1.call-update) | async-done | bytes 1048592 | tf_op jit(solution)/shard_map/psum | solution.py:162
  328.0 1.6 multiply_reduce_fusion
  329.6 1.1 fusion.65
  330.8 19.4 %all_to_all.96 = bf16[128,2,128]{2,1,0:T(2,128)(2,1)S(1)} all-to-all(bf16[128,2,128]{2,1,0:T(2,128)(2,1)S(1)} %copy.169), channel_id=1, replica_groups=mesh['dp'=32,'mp'=8] {'dp'}, dimensions={0} | all-to-all | bytes 131072 | tf_op jit(solution)/shard_map/all_to_all | solution.py:30
  350.3 12.9 %all_to_all.97 = bf16[8,4,64,128]{3,2,1,0:T(8,128)(2,1)S(1)} all-to-all(bf16[8,4,64,128]{3,2,1,0:T(8,128)(2,1)S(1)} %stack.28), channel_id=1, replica_groups=mesh['dp'=32,'mp'=8] {'mp'}, dimensions={0} | all-to-all | bytes 1048576 | tf_op jit(solution)/shard_map/all_to_all | solution.py:17
  363.3 1.9 multiply_convert_fusion.1
  365.9 1.4 convolution_add_fusion.1
  368.2 34.0 %reduce-scatter.15.cloned.1.call-done = f32[4,64,128]{2,1,0:T(8,128)} async-done(((f32[4,64,1024]{2,1,0:T(8,128)}), f32[4,64,128]{2,1,0:T(8,128)}) %reduce-scatter.15.cloned.1.call-update) | async-done | bytes 131088 | tf_op jit(solution)/shard_map/reduce_scatter | solution.py:26
  402.2 1.0 fusion.57
  403.2 17.1 %psum.38 = f32[4,64]{1,0:T(4,128)S(1)} all-reduce(f32[4,64]{1,0:T(4,128)S(1)} %fusion.57), channel_id=1, replica_groups=mesh['dp'=32,'mp'=8] {'mp'}, use_global_device_ids=true, to_apply=%region_16.17 | all-reduce | flops 256 | bytes 2048 | tf_op jit(solution)/shard_map/psum | solution.py:57
  420.3 1.1 fusion.72
  421.5 11.7 %all_to_all.98 = bf16[8,4,64,128]{3,2,1,0:T(8,128)(2,1)S(1)} all-to-all(bf16[8,4,64,128]{3,2,1,0:T(8,128)(2,1)S(1)} %stack.29), channel_id=1, replica_groups=mesh['dp'=32,'mp'=8] {'mp'}, dimensions={0} | all-to-all | bytes 1048576 | tf_op jit(solution)/shard_map/all_to_all | solution.py:17
  433.2 1.9 convolution_convert_fusion.5
  435.1 1.6 copy.214
  436.7 1.8 fusion.76
  438.5 1.9 convolution_convert_fusion.1
  440.4 2.3 convolution_convert_fusion.3
  442.7 2.2 convolution_convert_fusion.2
  444.9 1.6 copy.183
  446.5 1.6 copy.182
  448.2 1.6 copy.181
  449.8 2.7 convolution_bitcast_fusion.1
  452.7 2.7 bitcast_dynamic-update-slice_fusion.3
  455.4 2.0 fusion.2
  457.4 2.8 bitcast_dynamic-update-slice_fusion.2
  460.3 2.6 bitcast_dynamic-update-slice_fusion.1
  462.9 1.8 bitcast_dynamic-update-slice_fusion
  464.7 9.2 %copy.204 = f32[1024,2048]{1,0:T(8,128)} copy(f32[1024,2048]{0,1:T(8,128)} %bitcast_dynamic-update-slice_fusion) | data formatting | bytes 16777216
  474.9 19.2 %reduce-scatter.17.cloned.1.call-done = f32[4,64,128]{2,1,0:T(8,128)} async-done(((f32[4,64,1024]{2,1,0:T(8,128)}), f32[4,64,128]{2,1,0:T(8,128)}) %reduce-scatter.17.cloned.1.call-update) | async-done | bytes 131088 | tf_op jit(solution)/shard_map/reduce_scatter | solution.py:26
  494.1 1.0 multiply_reduce_fusion.2
  495.2 17.2 %all-reduce.1 = (f32[128,2]{0,1:T(2,128)S(1)}, f32[4,64]{1,0:T(4,128)S(1)}) all-reduce(f32[128,2]{0,1:T(2,128)S(1)} %copy-done.30, f32[4,64]{1,0:T(4,128)S(1)} %get-tuple-element.46), channel_id=1, replica_groups=mesh['dp'=32,'mp'=8] {'mp'}, use_global_device_ids=true, to_apply=%region_10.11 | all-reduce | flops 512 | bytes 4096 | tf_op jit(solution)/shard_map/psum | solution.py:143
  512.8 19.6 %all_to_all.99 = bf16[4,64,128]{2,0,1:T(4,128)(2,1)S(1)} all-to-all(bf16[4,64,128]{2,0,1:T(4,128)(2,1)S(1)} %concatenate.12.clone), channel_id=1, replica_groups=mesh['dp'=32,'mp'=8] {'dp'}, dimensions={1} | all-to-all | bytes 131072 | tf_op jit(solution)/shard_map/all_to_all | solution.py:34
  533.3 6.1 all-to-all-start.9
  540.4 7.6 %all-to-all-done.9 = bf16[8,128,2,128]{3,1,2,0:T(8,128)(2,1)S(1)} async-done(((bf16[8,128,2,128]{3,1,2,0:T(8,128)(2,1)}), bf16[8,128,2,128]{3,1,2,0:T(8,128)(2,1)S(1)}, u32[]{:S(2)}, u32[]{:S(2)}) %all-to-all-start.9) | async-done | bytes 524320 | tf_op jit(solution)/shard_map/all_to_all | solution.py:17
  548.0 1.3 convolution_add_fusion
  549.2 104.7 %reduce-scatter.19.cloned.1.call-done = f32[32,2048]{1,0:T(8,128)} async-done(((f32[1024,2048]{1,0:T(8,128)}), f32[32,2048]{1,0:T(8,128)}) %reduce-scatter.19.cloned.1.call-update) | async-done | bytes 262160
  655.6 1.3 slice.51
  657.0 1.6 fusion.101
  (134 shorter events, 19.0 us)
Async XLA Ops:
  7.2 144.2 %copy-start = (bf16[1024,512]{1,0:T(8,128)(2,1)S(1)}, bf16[1024,512]{1,0:T(8,128)(2,1)}, u32[]{:S(2)}) copy-start(bf16[1024,512]{1,0:T(8,128)(2,1)} %param.25) | copy-start | bytes 3145732
  7.2 88.3 %copy-start.10 = (bf16[1024,128]{1,0:T(8,128)(2,1)S(1)}, bf16[1024,128]{1,0:T(8,128)(2,1)}, u32[]{:S(2)}) copy-start(bf16[1024,128]{1,0:T(8,128)(2,1)} %param.22) | copy-start | bytes 786436
  7.2 47.3 %reduce-scatter.9.cloned.1.call-start = ((), (), s32[]{:S(2)}) async-start(), calls=%async_computation.16 | async-start | bytes 1179648 | tf_op jit(solution)/shard_map/reduce_scatter | solution.py:26
  10.4 129.0 %copy-start.29 = (bf16[1024]{0:T(1024)(128)(2,1)S(1)}, bf16[1024]{0:T(1024)(128)(2,1)}, u32[]{:S(2)}) copy-start(bf16[1024]{0:T(1024)(128)(2,1)} %param.19) | copy-start | bytes 6148
  56.1 20.0 %all-to-all-start = ((bf16[128,2,128]{2,1,0:T(2,128)(2,1)}), bf16[128,2,128]{2,1,0:T(2,128)(2,1)S(1)}, u32[]{:S(2)}, u32[]{:S(2)}) async-start(bf16[128,2,128]{2,1,0:T(2,128)(2,1)} %copy.156), calls=%async_computation.1 | async-start | bytes 131072 | tf_op jit(solution)/shard_map/all_to_all | solution.py:30
  77.7 14.3 %all-to-all-start.1 = ((bf16[8,4,64,128]{3,2,1,0:T(8,128)(2,1)}), bf16[8,4,64,128]{3,2,1,0:T(8,128)(2,1)S(1)}, u32[]{:S(2)}, u32[]{:S(2)}) async-start(bf16[8,4,64,128]{3,2,1,0:T(8,128)(2,1)} %stack.24), calls=%async_computation.2 | async-start | bytes 1048576 | tf_op jit(solution)/shard_map/all_to_all | solution.py:17
  83.4 48.0 %reduce-scatter.11.cloned.1.call-start = ((), (), s32[]{:S(2)}) async-start(), calls=%async_computation.17 | async-start | bytes 1179648 | tf_op jit(solution)/shard_map/reduce_scatter | solution.py:26
  84.1 62.7 %copy-start.24 = (f32[1024]{0:T(1024)}, f32[1024]{0:T(1024)S(1)}, u32[]{:S(2)}) copy-start(f32[1024]{0:T(1024)S(1)} %convert_element_type.150) | copy-start | bytes 12292
  84.1 62.7 %copy-start.22 = (pred[64,64]{0,1:T(8,128)(4,1)}, pred[64,64]{0,1:T(8,128)(4,1)S(1)}, u32[]{:S(2)}) copy-start(pred[64,64]{0,1:T(8,128)(4,1)S(1)} %iota_compare_fusion.3) | copy-start | bytes 12292
  92.8 54.0 %copy-start.20 = (f32[4,64]{1,0:T(4,128)}, f32[4,64]{1,0:T(4,128)S(1)}, u32[]{:S(2)}) copy-start(f32[4,64]{1,0:T(4,128)S(1)} %get-tuple-element.61) | copy-start | bytes 3076
  94.6 38.7 %copy-start.14 = (bf16[4,64,1,128]{1,3,0,2:T(8,128)(2,1)}, bf16[4,64,1,128]{1,3,0,2:T(8,128)(2,1)S(1)}, u32[]{:S(2)}) copy-start(bf16[4,64,1,128]{1,3,0,2:T(8,128)(2,1)S(1)} %copy.213) | copy-start | bytes 196612
  94.7 56.6 %copy-start.7 = (bf16[4,64,2,64]{3,2,1,0:T(2,128)(2,1)}, bf16[4,64,2,64]{3,2,1,0:T(2,128)(2,1)S(1)}, u32[]{:S(2)}) copy-start(bf16[4,64,2,64]{3,2,1,0:T(2,128)(2,1)S(1)} %reshape_squeeze.9) | copy-start | bytes 196612
  94.9 38.4 %copy-start.15 = (bf16[4,64,1,128]{1,3,0,2:T(8,128)(2,1)}, bf16[4,64,1,128]{1,3,0,2:T(8,128)(2,1)S(1)}, u32[]{:S(2)}) copy-start(bf16[4,64,1,128]{1,3,0,2:T(8,128)(2,1)S(1)} %copy.212) | copy-start | bytes 196612
  95.2 38.1 %copy-start.32 = (f32[4,2,64,64]{2,3,1,0:T(8,128)}, f32[4,2,64,64]{2,3,1,0:T(8,128)S(1)}, u32[]{:S(2)}) copy-start(f32[4,2,64,64]{2,3,1,0:T(8,128)S(1)} %get-tuple-element.67) | copy-start | bytes 393220
  95.2 50.9 %copy-start.33 = (f32[4,2,64]{2,1,0:T(2,128)}, f32[4,2,64]{2,1,0:T(2,128)S(1)}, u32[]{:S(2)}) copy-start(f32[4,2,64]{2,1,0:T(2,128)S(1)} %get-tuple-element.66) | copy-start | bytes 6148
  95.5 55.9 %copy-start.8 = (bf16[4,2,64,64]{3,2,1,0:T(8,128)(2,1)}, bf16[4,2,64,64]{3,2,1,0:T(8,128)(2,1)S(1)}, u32[]{:S(2)}) copy-start(bf16[4,2,64,64]{3,2,1,0:T(8,128)(2,1)S(1)} %convolution_convert_fusion.4) | copy-start | bytes 196612
  133.3 12.8 %all-to-all-start.2 = ((bf16[8,4,64,128]{3,2,1,0:T(8,128)(2,1)}), bf16[8,4,64,128]{3,2,1,0:T(8,128)(2,1)S(1)}, u32[]{:S(2)}, u32[]{:S(2)}) async-start(bf16[8,4,64,128]{3,2,1,0:T(8,128)(2,1)} %stack.25), calls=%async_computation.4 | async-start | bytes 1048576 | tf_op jit(solution)/shard_map/all_to_all | solution.py:17
  139.4 54.5 %reduce-scatter.13.cloned.1.call-start = ((), (), s32[]{:S(2)}) async-start(), calls=%async_computation.18 | async-start | bytes 1179648 | tf_op jit(solution)/shard_map/reduce_scatter | solution.py:26
  139.4 13.5 %copy-start.25 = (f32[1024]{0:T(1024)}, f32[1024]{0:T(1024)S(1)}, u32[]{:S(2)}) copy-start(f32[1024]{0:T(1024)S(1)} %convert_element_type.162) | copy-start | bytes 12292
  146.9 6.0 copy-start.16
  146.9 58.5 %copy-start.28 = (bf16[1024]{0:T(1024)(128)(2,1)S(1)}, bf16[1024]{0:T(1024)(128)(2,1)}, u32[]{:S(2)}) copy-start(bf16[1024]{0:T(1024)(128)(2,1)} %param.20) | copy-start | bytes 6148
  146.9 75.1 %copy-start.31 = (s32[2]{0:T(128)S(1)}, s32[2]{0:T(128)}, u32[]{:S(2)}) copy-start(s32[2]{0:T(128)} %param.15) | copy-start | bytes 28
  148.6 2.8 copy-start.34
  148.6 82.8 %copy-start.1 = (bf16[2,128,1024]{2,1,0:T(8,128)(2,1)S(1)}, bf16[2,128,1024]{2,1,0:T(8,128)(2,1)}, u32[]{:S(2)}) copy-start(bf16[2,128,1024]{2,1,0:T(8,128)(2,1)} %param.16) | copy-start | bytes 1572868
  195.5 19.8 %all-to-all-start.3 = ((bf16[4,64,128]{2,0,1:T(4,128)(2,1)}), bf16[4,64,128]{2,0,1:T(4,128)(2,1)S(1)}, u32[]{:S(2)}, u32[]{:S(2)}) async-start(bf16[4,64,128]{2,0,1:T(4,128)(2,1)} %copy.165), calls=%async_computation.6 | async-start | bytes 131072 | tf_op jit(solution)/shard_map/all_to_all | solution.py:34
  216.3 14.4 %all-to-all-start.4 = ((bf16[8,128,2,128]{3,1,2,0:T(8,128)(2,1)}), bf16[8,128,2,128]{3,1,2,0:T(8,128)(2,1)S(1)}, u32[]{:S(2)}, u32[]{:S(2)}) async-start(bf16[8,128,2,128]{3,1,2,0:T(8,128)(2,1)} %stack.27), calls=%async_computation.7 | async-start | bytes 1048576 | tf_op jit(solution)/shard_map/all_to_all | solution.py:17
  222.0 106.0 %all-reduce.4.cloned.1.call-start = ((), (), s32[]{:S(2)}) async-start(), calls=%async_computation.19 | async-start | bytes 2097152 | tf_op jit(solution)/shard_map/psum | solution.py:162
  231.4 1.6 copy-start.26
  252.2 150.0 %reduce-scatter.15.cloned.1.call-start = ((), (), s32[]{:S(2)}) async-start(), calls=%async_computation.20 | async-start | bytes 1179648 | tf_op jit(solution)/shard_map/reduce_scatter | solution.py:26
  253.3 167.0 %copy-start.17 = (f32[4,64]{1,0:T(4,128)S(1)}, f32[4,64]{1,0:T(4,128)}, u32[]{:S(2)}) copy-start(f32[4,64]{1,0:T(4,128)} %copy-done.16) | copy-start | bytes 3076
  253.3 167.0 %copy-start.18 = (f32[4,64]{1,0:T(4,128)S(1)}, f32[4,64]{1,0:T(4,128)}, u32[]{:S(2)}) copy-start(f32[4,64]{1,0:T(4,128)} %get-tuple-element.62) | copy-start | bytes 3076
  328.0 37.2 %copy-start.4 = (bf16[1024,512]{1,0:T(8,128)(2,1)S(1)}, bf16[1024,512]{1,0:T(8,128)(2,1)}, u32[]{:S(2)}) copy-start(bf16[1024,512]{1,0:T(8,128)(2,1)} %param.23) | copy-start | bytes 3145732
  328.0 37.9 %copy-start.5 = (bf16[1024,512]{1,0:T(8,128)(2,1)S(1)}, bf16[1024,512]{1,0:T(8,128)(2,1)}, u32[]{:S(2)}) copy-start(bf16[1024,512]{1,0:T(8,128)(2,1)} %param.24) | copy-start | bytes 3145732
  363.3 1.9 copy-start.2
  365.2 0.7 copy-start.11
  365.2 56.2 %copy-start.9 = (bf16[4,64,512]{2,1,0:T(8,128)(2,1)}, bf16[4,64,512]{2,1,0:T(8,128)(2,1)S(1)}, u32[]{:S(2)}) copy-start(bf16[4,64,512]{2,1,0:T(8,128)(2,1)S(1)} %get-tuple-element.51) | copy-start | bytes 786436
  367.4 126.8 %reduce-scatter.17.cloned.1.call-start = ((), (), s32[]{:S(2)}) async-start(), calls=%async_computation.21 | async-start | bytes 1179648 | tf_op jit(solution)/shard_map/reduce_scatter | solution.py:26
  452.5 201.5 %reduce-scatter.19.cloned.1.call-start = ((), (), s32[]{:S(2)}) async-start(), calls=%async_computation.22 | async-start | bytes 8650752
  452.7 7.5 %copy-start.12 = (bf16[4,64,512]{2,1,0:T(8,128)(2,1)S(1)}, bf16[4,64,512]{2,1,0:T(8,128)(2,1)}, u32[]{:S(2)}) copy-start(bf16[4,64,512]{2,1,0:T(8,128)(2,1)} %copy-done.11) | copy-start | bytes 786436
  452.7 10.2 %copy-start.3 = (bf16[8,4,64,128]{3,2,1,0:T(8,128)(2,1)S(1)}, bf16[8,4,64,128]{3,2,1,0:T(8,128)(2,1)}, u32[]{:S(2)}) copy-start(bf16[8,4,64,128]{3,2,1,0:T(8,128)(2,1)} %copy-done.2) | copy-start | bytes 1572868
  473.8 0.9 copy-start.21
  473.8 1.0 copy-start.19
  473.8 21.3 %copy-start.30 = (f32[128,2]{0,1:T(2,128)S(1)}, f32[128,2]{0,1:T(2,128)}, u32[]{:S(2)}) copy-start(f32[128,2]{0,1:T(2,128)} %get-tuple-element.43) | copy-start | bytes 3076
  473.8 38.6 %copy-start.6 = (f32[4,64,128]{2,1,0:T(8,128)S(1)}, f32[4,64,128]{2,1,0:T(8,128)}, u32[]{:S(2)}) copy-start(f32[4,64,128]{2,1,0:T(8,128)} %get-tuple-element.58) | copy-start | bytes 393220
  473.9 65.5 %copy-start.13 = (f32[2,128,128]{1,2,0:T(8,128)S(1)}, f32[2,128,128]{1,2,0:T(8,128)}, u32[]{:S(2)}) copy-start(f32[2,128,128]{1,2,0:T(8,128)} %get-tuple-element.70) | copy-start | bytes 393220
  473.9 65.5 %copy-start.23 = (f32[128,2]{0,1:T(2,128)S(1)}, f32[128,2]{0,1:T(2,128)}, u32[]{:S(2)}) copy-start(f32[128,2]{0,1:T(2,128)} %multiply_divide_fusion) | copy-start | bytes 3076
  473.9 65.5 %copy-start.27 = (f32[128,2]{0,1:T(2,128)S(1)}, f32[128,2]{0,1:T(2,128)}, u32[]{:S(2)}) copy-start(f32[128,2]{0,1:T(2,128)} %copy-done.26) | copy-start | bytes 3076
  533.3 14.7 %all-to-all-start.9 = ((bf16[8,128,2,128]{3,1,2,0:T(8,128)(2,1)}), bf16[8,128,2,128]{3,1,2,0:T(8,128)(2,1)S(1)}, u32[]{:S(2)}, u32[]{:S(2)}) async-start(bf16[8,128,2,128]{3,1,2,0:T(8,128)(2,1)} %stack.35), calls=%async_computation.14 | async-start | bytes 1048576 | tf_op jit(solution)/shard_map/all_to_all | solution.py:17
Sparse Core Ops, SparseCore 0:
  11.1 43.3 reduce-scatter.8
  96.9 34.4 reduce-scatter.10
  153.0 40.8 reduce-scatter.12
  252.3 75.6 all-reduce.3
  367.5 34.5 reduce-scatter.14
  452.6 41.4 reduce-scatter.16
  498.5 155.3 reduce-scatter.18
